TPU v7x, 32 devices: a whole 2x2x4 slice. The times are simulated.
32 devices in a mesh: rep: 8 (over z, x), exp: 4 (over y, core).
Axes of the slice: x: 2, y: 2, z: 4, core: 2. Of those that a mesh axis runs over, the one named last changes fastest.
Arguments:
- expert_ids: int32 [8, 512, 8], P('rep', 'exp'), may hold values from 0 to 15, as said below
- route_weights: bfloat16 [8, 512, 8], P('rep', 'exp'), may hold values from 0.049804688 to 0.59765625
- out_grad: bfloat16 [8, 512, 1024], P('rep', 'exp'), may hold values from -6 to 6
- saved_inputs: bfloat16 [8, 4, 32, 1024], P('rep', 'exp'), may hold values from -6 to 6
- gate_weight: bfloat16 [4, 1024, 384], P('exp', 'rep'), may hold values from -0.1875 to 0.1875
- up_weight: bfloat16 [4, 1024, 384], P('exp', 'rep'), may hold values from -0.1875 to 0.1875
- down_weight: bfloat16 [4, 1024, 384], P('exp', 'rep'), may hold values from -0.3125 to 0.3125
Outputs:
- input_grad: bfloat16 [8, 512, 1024], P('rep', 'exp')
- route_grad: bfloat16 [8, 512, 8], P('rep', 'exp')
- gate_grad: float32 [4, 1024, 384], P('exp', 'rep')
- up_grad: float32 [4, 1024, 384], P('exp', 'rep')
- down_grad: float32 [4, 1024, 384], P('exp', 'rep')
Inputs may be any that keep to these rules, and one draw needn't show every extreme that they name: `expert_ids`: each row names 8 different experts. Within each aligned block of 128 rows of one replica, an expert e with e % 4 == 0 is named at most 8 times; for every replica, some such expert is named exactly 8 times in each of its blocks.
All inputs are finite; a program needn't handle non-finite values.
Results may differ from a plain program's by a relative error of at most 0.014.
Values may be sent and summed in bfloat16 or wider, within the bound.
No kernel may reach another device: no remote copies, remote signals or barrier semaphores. Data moves between devices by JAX's collectives and lax.ppermute only.
A program may use at most 64 MiB of HBM per device.

v0:
```python
import jax
import jax.numpy as jnp
from jax import lax
from jax.sharding import PartitionSpec as P

TOPK = 8
EXP_DEV = 4


def slot_table(block_ids, slot_count, owners):
    flat_ids = block_ids.reshape(-1)
    chosen = flat_ids % EXP_DEV == 0
    owner_of = flat_ids // EXP_DEV
    capacity = slot_count // owners
    onehot = ((owner_of[:, None] == jnp.arange(owners)[None, :]) & chosen[:, None]).astype(
        jnp.int32
    )
    earlier = jnp.cumsum(onehot, axis=0) - onehot
    position = jnp.sum(earlier * onehot, axis=1)
    slot_of = jnp.where(chosen, owner_of * capacity + position, -1)
    return slot_of[None, :] == jnp.arange(slot_count)[:, None]


def first_contract(left, right):
    return lax.dot_general(
        left, right, (((0,), (0,)), ((), ())), preferred_element_type=jnp.float32
    )


def second_contract(left, right):
    return lax.dot_general(
        left, right, (((1,), (1,)), ((), ())), preferred_element_type=jnp.float32
    )


def body(expert_ids, route_weights, out_grad, saved_inputs, gate_weight, up_weight, down_weight):
    owners = lax.axis_size("exp")
    replicas = lax.axis_size("rep")
    tokens_here = out_grad.shape[1]
    features = out_grad.shape[2]
    hidden_width = gate_weight.shape[2]
    slot_count = saved_inputs.shape[2]
    capacity = slot_count // owners
    placed = slot_table(expert_ids[0], slot_count, owners)
    weights_flat = route_weights[0].reshape(-1)
    slot_scale = jnp.sum(
        jnp.where(placed, weights_flat[None, :], jnp.zeros((), weights_flat.dtype)), axis=1
    )
    token_hits = jnp.any(placed.reshape(slot_count, tokens_here, TOPK), axis=2)
    token_of = jnp.sum(jnp.where(token_hits, jnp.arange(tokens_here)[None, :], 0), axis=1)
    is_live = jnp.any(token_hits, axis=1)
    routed = jnp.where(is_live[:, None], out_grad[0][token_of], jnp.zeros((), jnp.bfloat16))
    arrived, arrived_scale = (
        lax.all_to_all(
            routed.reshape(owners, capacity, features),
            "exp",
            split_axis=0,
            concat_axis=0,
            tiled=True,
        ),
        lax.all_to_all(
            slot_scale.reshape(owners, capacity), "exp", split_axis=0, concat_axis=0, tiled=True
        ),
    )
    full_gate, full_up, full_down = (
        lax.all_gather(gate_weight[0], "rep", axis=0, tiled=True),
        lax.all_gather(up_weight[0], "rep", axis=0, tiled=True),
        lax.all_gather(down_weight[0], "rep", axis=0, tiled=True),
    )
    grad_rows = arrived.reshape(slot_count, features)
    scale_col = arrived_scale.reshape(slot_count, 1).astype(jnp.float32)
    inputs_here = saved_inputs[0, 0]
    pre_gate = jnp.dot(inputs_here, full_gate, preferred_element_type=jnp.float32)
    pre_up = jnp.dot(inputs_here, full_up, preferred_element_type=jnp.float32)
    sigmoid_gate = jax.nn.sigmoid(pre_gate)
    activated = pre_gate * sigmoid_gate
    hidden = (activated * pre_up).astype(jnp.bfloat16)
    raw_grad = jnp.dot(grad_rows, full_down, preferred_element_type=jnp.float32)
    slot_route = jnp.sum(hidden.astype(jnp.float32) * raw_grad, axis=1).astype(jnp.bfloat16)
    hidden_grad = scale_col * raw_grad
    scaled_rows = (scale_col * grad_rows.astype(jnp.float32)).astype(jnp.bfloat16)
    gate_delta = (
        hidden_grad * pre_up * sigmoid_gate * (1.0 + pre_gate * (1.0 - sigmoid_gate))
    ).astype(jnp.bfloat16)
    up_delta = (hidden_grad * activated).astype(jnp.bfloat16)
    back_rows = (
        second_contract(gate_delta, full_gate) + second_contract(up_delta, full_up)
    ).astype(jnp.bfloat16)
    returned, returned_route = (
        lax.all_to_all(
            back_rows.reshape(owners, capacity, features),
            "exp",
            split_axis=0,
            concat_axis=0,
            tiled=True,
        ),
        lax.all_to_all(
            slot_route.reshape(owners, capacity), "exp", split_axis=0, concat_axis=0, tiled=True
        ),
    )
    returned_flat = returned.reshape(slot_count, features)
    route_flat = returned_route.reshape(slot_count)
    combined = jax.ops.segment_sum(
        jnp.where(is_live[:, None], returned_flat.astype(jnp.float32), 0.0),
        token_of,
        num_segments=tokens_here,
    )
    input_grad = combined.astype(jnp.bfloat16)[None]
    route_grad = jnp.sum(
        jnp.where(placed, route_flat[:, None], jnp.zeros((), jnp.bfloat16)), axis=0
    )
    route_grad = route_grad.reshape(1, tokens_here, TOPK)
    joined_share = lax.psum_scatter(
        jnp.concatenate(
            [
                jnp.concatenate(
                    [
                        first_contract(inputs_here, gate_delta),
                        first_contract(inputs_here, up_delta),
                    ],
                    axis=1,
                ),
                first_contract(scaled_rows, hidden),
            ],
            axis=1,
        ),
        "rep",
        scatter_dimension=0,
        tiled=True,
    )
    gate_share = joined_share[:, :hidden_width]
    up_share = joined_share[:, hidden_width : 2 * hidden_width]
    down_share = joined_share[:, 2 * hidden_width :]
    gate_grad = (gate_share / replicas)[None]
    up_grad = (up_share / replicas)[None]
    down_grad = (down_share / replicas)[None]
    return (input_grad, route_grad, gate_grad, up_grad, down_grad)


def solution(mesh):
    in_specs = (
        P("rep", "exp", None),
        P("rep", "exp", None),
        P("rep", "exp", None),
        P("rep", "exp", None, None),
        P("exp", "rep", None),
        P("exp", "rep", None),
        P("exp", "rep", None),
    )
    out_specs = (
        P("rep", "exp", None),
        P("rep", "exp", None),
        P("exp", "rep", None),
        P("exp", "rep", None),
        P("exp", "rep", None),
    )
    return jax.shard_map(body, mesh=mesh, in_specs=in_specs, out_specs=out_specs, check_vma=False)
```

profile of v0, /device:TPU:0, one launch (start us, length us, event | category | flops | bytes accessed | tf_op | source)
XLA Modules:
  0.0 239.1 jit_solution(11610807980264724344)
XLA Ops:
  7.2 0.0 copy-start
  7.2 0.0 copy-start.2
  7.2 0.0 copy-start.3
  7.2 0.8 copy.44
  8.0 0.1 reshape_squeeze.8
  8.1 0.1 reshape_squeeze.9
  8.2 0.0 copy-start.1
  8.3 1.1 reduce-window.6
  9.5 0.2 slice_reduce_fusion
  9.7 0.2 reduce-window.9
  9.9 0.1 add_bitcast_fusion
  10.0 0.1 reduce_sum.54
  10.1 0.1 fusion.23
  10.2 0.7 fusion.18
  10.9 0.1 select_reduce_fusion
  11.0 0.1 broadcast_in_dim.101
  11.1 0.0 copy-done
  11.1 0.6 gather_fusion
  11.7 0.7 bitcast_select_fusion
  12.4 4.2 %all-to-all-start.1 = ((bf16[4,8,1024]{2,1,0:T(8,128)(2,1)}), bf16[4,8,1024]{2,1,0:T(8,128)(2,1)S(1)}, u32[]{:S(2)}, u32[]{:S(2)}) async-start(bf16[4,8,1024]{2,1,0:T(8,128)(2,1)} %bitcast_select_fusion), calls=%async_computation.1 | async-start | bytes 131072 | tf_op jit(solution)/shard_map/all_to_all | solution.py:54
  16.7 0.0 copy-start.4
  16.7 0.0 reduce-scatter.2.cloned.1.call-start
  16.7 0.0 copy-done.2
  16.7 33.0 %all-gather.2 = bf16[1,1024,384]{2,1,0:T(8,128)(2,1)S(1)} all-gather(bf16[1,128,384]{2,1,0:T(8,128)(2,1)S(1)} %copy-done.2), channel_id=4, replica_groups=mesh['rep'=8,'exp'=4] {'rep'}, dimensions={1}, use_global_device_ids=true | all-gather | bytes 884736 | tf_op jit(solution)/shard_map/all_gather | solution.py:66
  49.7 0.0 copy-done.3
  49.7 0.0 copy-start.5
  49.7 32.4 %all-gather.1 = bf16[1,1024,384]{2,1,0:T(8,128)(2,1)S(1)} all-gather(bf16[1,128,384]{2,1,0:T(8,128)(2,1)S(1)} %copy-done.3), channel_id=3, replica_groups=mesh['rep'=8,'exp'=4] {'rep'}, dimensions={1}, use_global_device_ids=true | all-gather | bytes 884736 | tf_op jit(solution)/shard_map/all_gather | solution.py:67
  82.1 0.0 copy-done.1
  82.1 0.2 fusion.4
  82.3 0.2 fusion.7
  82.6 0.0 copy-done.4
  82.6 32.0 %all-gather = bf16[1,1024,384]{2,1,0:T(8,128)(2,1)S(1)} all-gather(bf16[1,128,384]{2,1,0:T(8,128)(2,1)S(1)} %copy-done.4), channel_id=2, replica_groups=mesh['rep'=8,'exp'=4] {'rep'}, dimensions={1}, use_global_device_ids=true | all-gather | bytes 884736 | tf_op jit(solution)/shard_map/all_gather | solution.py:68
  114.6 0.0 copy-done.5
  114.6 0.1 copy.48
  114.7 0.1 broadcast_in_dim.98
  114.8 0.0 all-to-all-done.1
  114.8 0.3 multiply_reduce_fusion
  115.1 0.1 convert_element_type.84
  115.2 7.2 %all_to_all.26 = bf16[4,1,8]{2,1,0:T(2,128)(2,1)S(1)} all-to-all(bf16[4,1,8]{2,1,0:T(2,128)(2,1)S(1)} %convert_element_type.84), channel_id=1, replica_groups=mesh['rep'=8,'exp'=4] {'exp'}, dimensions={0} | all-to-all | bytes 128 | tf_op jit(solution)/shard_map/all_to_all | solution.py:97
  122.4 0.1 broadcast_in_dim.106
  122.5 0.1 fusion.25
  122.7 0.1 all_to_all.21
  122.7 6.1 %all_to_all.27 = bf16[4,1,8]{2,1,0:T(2,128)(2,1)S(1)} all-to-all(bf16[4,1,8]{2,1,0:T(2,128)(2,1)S(1)} %all_to_all.21), channel_id=1, replica_groups=mesh['rep'=8,'exp'=4] {'exp'}, dimensions={0} | all-to-all | bytes 128 | tf_op jit(solution)/shard_map/all_to_all | solution.py:61
  128.9 0.1 reshape.228
  128.9 0.1 multiply_convert_fusion.3
  129.0 0.4 convolution_bitcast_fusion
  129.4 0.4 convolution_bitcast_fusion.1
  129.8 0.4 fusion.26
  130.2 2.5 %pad_maximum_fusion = f32[1024,1152]{0,1:T(8,128)} fusion(f32[1024,384]{0,1:T(8,128)S(1)} %fusion.26, f32[1024,384]{0,1:T(8,128)S(1)} %convolution_bitcast_fusion, f32[1024,384]{0,1:T(8,128)S(1)} %convolution_bitcast_fusion.1), kind=kLoop, calls=%fused_computation.2 | loop fusion | flops 2359296 | bytes 9437184 | tf_op jit(solution)/shard_map/concatenate | solution.py:114
  132.7 0.0 reduce-scatter.2.cloned.1.call-update
  132.8 0.3 fusion.2
  133.1 1.0 fusion.1
  134.1 3.3 %all-to-all-start.2 = ((bf16[4,8,1024]{2,1,0:T(8,128)(2,1)}), bf16[4,8,1024]{2,1,0:T(8,128)(2,1)S(1)}, u32[]{:S(2)}, u32[]{:S(2)}) async-start(bf16[4,8,1024]{2,1,0:T(8,128)(2,1)} %fusion.1), calls=%async_computation.2 | async-start | bytes 131072 | tf_op jit(solution)/shard_map/all_to_all | solution.py:90
  137.4 0.1 reshape.227
  137.5 0.7 copy.51
  138.1 3.3 %all-to-all-done.2 = bf16[4,8,1024]{2,1,0:T(8,128)(2,1)S(1)} async-done(((bf16[4,8,1024]{2,1,0:T(8,128)(2,1)}), bf16[4,8,1024]{2,1,0:T(8,128)(2,1)S(1)}, u32[]{:S(2)}, u32[]{:S(2)}) %all-to-all-start.2) | async-done | bytes 65568 | tf_op jit(solution)/shard_map/all_to_all | solution.py:90
  141.5 1.0 scatter_custom_fusion
  142.5 0.7 convert_bitcast_fusion
  143.3 85.4 %reduce-scatter.2.cloned.1.call-done = f32[128,1152]{0,1:T(8,128)} async-done(((f32[1024,1152]{0,1:T(8,128)}), f32[128,1152]{0,1:T(8,128)}) %reduce-scatter.2.cloned.1.call-update) | async-done | bytes 589840 | tf_op jit(solution)/shard_map/reduce_scatter | solution.py:113
  228.6 1.2 fusion.13
  229.8 0.8 copy.54
  230.6 0.8 copy.53
  231.4 0.8 copy.52
  (12 shorter events, 0.2 us)
Async XLA Ops:
  7.2 3.9 %copy-start = (bf16[1,128,1024]{2,1,0:T(8,128)(2,1)S(1)}, bf16[1,128,1024]{2,1,0:T(8,128)(2,1)}, u32[]{:S(2)}) copy-start(bf16[1,128,1024]{2,1,0:T(8,128)(2,1)} %param.9) | copy-start | bytes 786436
  7.2 9.5 %copy-start.2 = (bf16[1,128,384]{2,1,0:T(8,128)(2,1)S(1)}, bf16[1,128,384]{2,1,0:T(8,128)(2,1)}, u32[]{:S(2)}) copy-start(bf16[1,128,384]{2,1,0:T(8,128)(2,1)} %param.11) | copy-start | bytes 294916
  7.2 42.5 %copy-start.3 = (bf16[1,128,384]{2,1,0:T(8,128)(2,1)S(1)}, bf16[1,128,384]{2,1,0:T(8,128)(2,1)}, u32[]{:S(2)}) copy-start(bf16[1,128,384]{2,1,0:T(8,128)(2,1)} %param.12) | copy-start | bytes 294916
  8.2 73.9 %copy-start.1 = (bf16[1,1,32,1024]{3,2,1,0:T(8,128)(2,1)S(1)}, bf16[1,1,32,1024]{3,2,1,0:T(8,128)(2,1)}, u32[]{:S(2)}) copy-start(bf16[1,1,32,1024]{3,2,1,0:T(8,128)(2,1)} %param.10) | copy-start | bytes 196612
  12.4 102.4 %all-to-all-start.1 = ((bf16[4,8,1024]{2,1,0:T(8,128)(2,1)}), bf16[4,8,1024]{2,1,0:T(8,128)(2,1)S(1)}, u32[]{:S(2)}, u32[]{:S(2)}) async-start(bf16[4,8,1024]{2,1,0:T(8,128)(2,1)} %bitcast_select_fusion), calls=%async_computation.1 | async-start | bytes 131072 | tf_op jit(solution)/shard_map/all_to_all | solution.py:54
  16.7 65.9 %copy-start.4 = (bf16[1,128,384]{2,1,0:T(8,128)(2,1)S(1)}, bf16[1,128,384]{2,1,0:T(8,128)(2,1)}, u32[]{:S(2)}) copy-start(bf16[1,128,384]{2,1,0:T(8,128)(2,1)} %param.13) | copy-start | bytes 294916
  16.7 211.9 %reduce-scatter.2.cloned.1.call-start = ((), (), s32[]{:S(2)}) async-start(), calls=%async_computation.5 | async-start | bytes 5308416 | tf_op jit(solution)/shard_map/reduce_scatter | solution.py:113
  49.7 64.8 %copy-start.5 = (bf16[1,128,8]{1,2,0:T(8,128)(2,1)S(1)}, bf16[1,128,8]{1,2,0:T(8,128)(2,1)}, u32[]{:S(2)}) copy-start(bf16[1,128,8]{1,2,0:T(8,128)(2,1)} %param.8) | copy-start | bytes 6148
  134.1 7.4 %all-to-all-start.2 = ((bf16[4,8,1024]{2,1,0:T(8,128)(2,1)}), bf16[4,8,1024]{2,1,0:T(8,128)(2,1)S(1)}, u32[]{:S(2)}, u32[]{:S(2)}) async-start(bf16[4,8,1024]{2,1,0:T(8,128)(2,1)} %fusion.1), calls=%async_computation.2 | async-start | bytes 131072 | tf_op jit(solution)/shard_map/all_to_all | solution.py:90
Sparse Core Ops, SparseCore 0:
  132.9 95.7 reduce-scatter.1
where the time goes:
time: 240 us; the launch traced here: 239 us
  blocking collectives  111 us (46%)
  waiting for transfers between devices  88.7 us (37%)
  between operations  14.2 us (6%)
  other arithmetic  8.79 us (4%)
  starting transfers between devices  7.52 us (3%)
  local copies, waits for them, and re-layouts  5.86 us (2%)
  matrix products  3.3 us (1%)
    reduce_scatter x1, waiting for transfers between devices, body(): lax.psum_scatter(jnp.concatenate([jnp.concatenate([first_contract(inputs_...  85.4 us
    all_gather x1, blocking collectives, body(): lax.all_gather(gate_weight[0], 'rep', axis=0, tiled=True)  33 us
    all_gather x1, blocking collectives, body(): lax.all_gather(up_weight[0], 'rep', axis=0, tiled=True)  32.4 us
    all_gather x1, blocking collectives, body(): lax.all_gather(down_weight[0], 'rep', axis=0, tiled=True)  32 us
    all_to_all x1, blocking collectives, body(): lax.all_to_all(slot_route.reshape(owners, capacity), 'exp', split_axis=0,...  7.19 us
    all_to_all x1, blocking collectives, body(): lax.all_to_all(slot_scale.reshape(owners, capacity), 'exp', split_axis=0,...  6.08 us
  transfers between devices with their start and end apart: 3, of which 2 were waited for; matrix products, arithmetic and copies ran while one was open for 2% of the time, Pallas kernels for 0%

commit v1 on v0

--- a/solution.py
+++ b/solution.py
@@ -5,6 +5,24 @@
 
 TOPK = 8
 EXP_DEV = 4
+
+
+def ring_gather(array, axis, dim):
+    ways, here, turn = (lax.axis_size(axis), lax.axis_index(axis), array.shape[dim])
+    lengths = [n * ways if d == dim else n for d, n in enumerate(array.shape)]
+    full = lax.dynamic_update_slice_in_dim(
+        jnp.zeros(lengths, array.dtype), array, here * turn, axis=dim
+    )
+    going_up = going_down = array
+    for far in range(1, ways // 2 + 1):
+        going_up = lax.ppermute(going_up, axis, [(d, (d + 1) % ways) for d in range(ways)])
+        full = lax.dynamic_update_slice_in_dim(full, going_up, (here - far) % ways * turn, axis=dim)
+        if 2 * far < ways:
+            going_down = lax.ppermute(going_down, axis, [(d, (d - 1) % ways) for d in range(ways)])
+            full = lax.dynamic_update_slice_in_dim(
+                full, going_down, (here + far) % ways * turn, axis=dim
+            )
+    return full
 
 
 def slot_table(block_ids, slot_count, owners):
@@ -63,7 +81,7 @@
         ),
     )
     full_gate, full_up, full_down = (
-        lax.all_gather(gate_weight[0], "rep", axis=0, tiled=True),
+        ring_gather(gate_weight[0], "rep", 0),
         lax.all_gather(up_weight[0], "rep", axis=0, tiled=True),
         lax.all_gather(down_weight[0], "rep", axis=0, tiled=True),
     )

time: 240 us -> 230 us (0.958)
  blocking collectives: 111 us -> 77.3 us
  starting transfers between devices: 7.52 us -> 22.2 us
  waiting for transfers between devices: 88.7 us -> 97.3 us
    all_gather x1 -> x0, blocking collectives: 33 us -> none  [body(): lax.all_gather(gate_weight[0], 'rep', axis=0, tiled=True)]
    ppermute x0 -> x7, starting transfers between devices: none -> 15.6 us  [the longest x3 12.5 us: ring_gather(): lax.ppermute(going_down, axis, [(d, (d - 1) % ways) for d in range(ways)])]
    ppermute x0 -> x7, waiting for transfers between devices: none -> 12.6 us  [the longest x4 12.6 us: ring_gather(): lax.ppermute(going_up, axis, [(d, (d + 1) % ways) for d in range(ways)])]
    reduce_scatter x1, waiting for transfers between devices: 85.4 us -> 81.3 us  [body(): lax.psum_scatter(jnp.concatenate([jnp.concatenate([first_contract(inputs_...]
  transfers between devices with their start and end apart: 3 -> 10, of which waited for: 2 -> 5; matrix products, arithmetic and copies ran while one was open for 2% -> 4% of each run, Pallas kernels for 0% -> 0%
where the time goes in v1:
time: 230 us; the launch traced here: 229 us
  waiting for transfers between devices  97.3 us (42%)
  blocking collectives  77.3 us (34%)
  starting transfers between devices  22.2 us (10%)
  between operations  14.5 us (6%)
  other arithmetic  8.79 us (4%)
  local copies, waits for them, and re-layouts  6.06 us (3%)
  matrix products  3.31 us (1%)
    reduce_scatter x1, waiting for transfers between devices, body(): lax.psum_scatter(jnp.concatenate([jnp.concatenate([first_contract(inputs_...  81.3 us
    all_gather x1, blocking collectives, body(): lax.all_gather(down_weight[0], 'rep', axis=0, tiled=True)  32.6 us
    all_gather x1, blocking collectives, body(): lax.all_gather(up_weight[0], 'rep', axis=0, tiled=True)  32.3 us
    ppermute x4, waiting for transfers between devices, ring_gather(): lax.ppermute(going_up, axis, [(d, (d + 1) % ways) for d in range(ways)])  12.6 us
    ppermute x3, starting transfers between devices, ring_gather(): lax.ppermute(going_down, axis, [(d, (d - 1) % ways) for d in range(ways)])  12.5 us
    all_to_all x1, blocking collectives, body(): lax.all_to_all(slot_route.reshape(owners, capacity), 'exp', split_axis=0,...  6.37 us
    all_to_all x1, blocking collectives, body(): lax.all_to_all(slot_scale.reshape(owners, capacity), 'exp', split_axis=0,...  6.08 us
  transfers between devices with their start and end apart: 10, of which 5 were waited for; matrix products, arithmetic and copies ran while one was open for 4% of the time, Pallas kernels for 0%

profile of v1, /device:TPU:0, one launch (start us, length us, event | category | flops | bytes accessed | tf_op | source)
XLA Modules:
  0.0 229.4 jit_solution(7685181578068588570)
XLA Ops:
  7.2 0.0 copy-start
  7.2 3.0 %collective-permute-start = (bf16[128,384]{1,0:T(8,128)(2,1)}, bf16[128,384]{1,0:T(8,128)(2,1)S(1)}, u32[]{:S(2)}, u32[]{:S(2)}) collective-permute-start(bf16[128,384]{1,0:T(8,128)(2,1)} %bitcast.102), channel_id=1, source_target_pairs={{0,4},{4,8},{8,12},{12,16},{16,20},{20,24},{24,28},{28,0},{1,5},{5... | collective-permute-start | bytes 294920 | tf_op jit(solution)/shard_map/ppermute | solution.py:18
  10.2 3.1 %collective-permute-start.1 = (bf16[128,384]{1,0:T(8,128)(2,1)}, bf16[128,384]{1,0:T(8,128)(2,1)S(1)}, u32[]{:S(2)}, u32[]{:S(2)}) collective-permute-start(bf16[128,384]{1,0:T(8,128)(2,1)} %bitcast.103), channel_id=1, source_target_pairs={{0,28},{4,0},{8,4},{12,8},{16,12},{20,16},{24,20},{28,24},{1,29},{... | collective-permute-start | bytes 294920 | tf_op jit(solution)/shard_map/ppermute | solution.py:21
  13.3 0.8 copy.44
  14.1 0.1 reshape_squeeze.8
  14.2 0.1 reshape_squeeze.9
  14.3 0.0 copy-start.1
  14.4 1.1 reduce-window.6
  15.5 0.2 slice_reduce_fusion
  15.7 0.2 reduce-window.9
  15.9 0.1 add_bitcast_fusion
  16.0 0.1 reduce_sum.54
  16.1 0.1 fusion.20
  16.2 0.7 fusion.15
  16.9 0.1 select_reduce_fusion
  17.1 0.1 broadcast_in_dim.104
  17.2 0.6 gather_fusion
  17.8 0.7 bitcast_select_fusion
  18.5 3.3 %all-to-all-start.1 = ((bf16[4,8,1024]{2,1,0:T(8,128)(2,1)}), bf16[4,8,1024]{2,1,0:T(8,128)(2,1)S(1)}, u32[]{:S(2)}, u32[]{:S(2)}) async-start(bf16[4,8,1024]{2,1,0:T(8,128)(2,1)} %bitcast_select_fusion), calls=%async_computation.1 | async-start | bytes 131072 | tf_op jit(solution)/shard_map/all_to_all | solution.py:72
  21.8 0.0 reduce-scatter.2.cloned.1.call-start
  21.9 0.0 copy-start.4
  21.9 32.3 %all-gather.1 = bf16[1,1024,384]{2,1,0:T(8,128)(2,1)S(1)} all-gather(bf16[1,128,384]{2,1,0:T(8,128)(2,1)S(1)} %copy-done.2), channel_id=3, replica_groups=mesh['rep'=8,'exp'=4] {'rep'}, dimensions={1}, use_global_device_ids=true | all-gather | bytes 884736 | tf_op jit(solution)/shard_map/all_gather | solution.py:85
  54.1 32.6 %all-gather = bf16[1,1024,384]{2,1,0:T(8,128)(2,1)S(1)} all-gather(bf16[1,128,384]{2,1,0:T(8,128)(2,1)S(1)} %copy-done.3), channel_id=2, replica_groups=mesh['rep'=8,'exp'=4] {'rep'}, dimensions={1}, use_global_device_ids=true | all-gather | bytes 884736 | tf_op jit(solution)/shard_map/all_gather | solution.py:86
  86.7 0.2 fusion.4
  86.9 0.1 broadcast_in_dim.107
  87.2 0.1 copy.48
  87.3 0.1 broadcast_in_dim.101
  87.5 0.0 collective-permute-done
  87.5 0.1 collective-permute-start.2
  87.5 0.0 collective-permute-done.1
  87.5 4.7 %collective-permute-start.3 = (bf16[128,384]{1,0:T(8,128)(2,1)S(1)}, bf16[128,384]{1,0:T(8,128)(2,1)S(1)}, u32[]{:S(2)}, u32[]{:S(2)}) collective-permute-start(bf16[128,384]{1,0:T(8,128)(2,1)S(1)} %collective-permute-done.1), channel_id=1, source_target_pairs={{0,28},{4,0},{8,4},{12,8},{16,12},{20,16},{24,20},{28,24},{1,29},{... | collective-permute-start | bytes 294920 | tf_op jit(solution)/shard_map/ppermute | solution.py:21
  92.3 2.8 %collective-permute-done.2 = bf16[128,384]{1,0:T(8,128)(2,1)S(1)} collective-permute-done((bf16[128,384]{1,0:T(8,128)(2,1)S(1)}, bf16[128,384]{1,0:T(8,128)(2,1)S(1)}, u32[]{:S(2)}, u32[]{:S(2)}) %collective-permute-start.2) | collective-permute-done | bytes 98336 | tf_op jit(solution)/shard_map/ppermute | solution.py:18
  95.1 4.7 %collective-permute-start.5 = (bf16[128,384]{1,0:T(8,128)(2,1)S(1)}, bf16[128,384]{1,0:T(8,128)(2,1)S(1)}, u32[]{:S(2)}, u32[]{:S(2)}) collective-permute-start(bf16[128,384]{1,0:T(8,128)(2,1)S(1)} %collective-permute-done.3), channel_id=1, source_target_pairs={{0,28},{4,0},{8,4},{12,8},{16,12},{20,16},{24,20},{28,24},{1,29},{... | collective-permute-start | bytes 294920 | tf_op jit(solution)/shard_map/ppermute | solution.py:21
  99.9 2.5 %collective-permute-done.4 = bf16[128,384]{1,0:T(8,128)(2,1)S(1)} collective-permute-done((bf16[128,384]{1,0:T(8,128)(2,1)S(1)}, bf16[128,384]{1,0:T(8,128)(2,1)S(1)}, u32[]{:S(2)}, u32[]{:S(2)}) %collective-permute-start.4) | collective-permute-done | bytes 98336 | tf_op jit(solution)/shard_map/ppermute | solution.py:18
  102.5 7.2 %collective-permute-done.6 = bf16[128,384]{1,0:T(8,128)(2,1)S(1)} collective-permute-done((bf16[128,384]{1,0:T(8,128)(2,1)S(1)}, bf16[128,384]{1,0:T(8,128)(2,1)S(1)}, u32[]{:S(2)}, u32[]{:S(2)}) %collective-permute-start.6) | collective-permute-done | bytes 98336 | tf_op jit(solution)/shard_map/ppermute | solution.py:18
  109.8 0.2 convolution_bitcast_fusion.2
  110.0 0.0 all-to-all-done.1
  110.0 0.3 multiply_reduce_fusion
  110.4 0.1 convert_element_type.84
  110.5 6.4 %all_to_all.26 = bf16[4,1,8]{2,1,0:T(2,128)(2,1)S(1)} all-to-all(bf16[4,1,8]{2,1,0:T(2,128)(2,1)S(1)} %convert_element_type.84), channel_id=1, replica_groups=mesh['rep'=8,'exp'=4] {'exp'}, dimensions={0} | all-to-all | bytes 128 | tf_op jit(solution)/shard_map/all_to_all | solution.py:115
  116.8 0.1 broadcast_in_dim.110
  116.9 0.1 fusion.22
  117.1 0.1 all_to_all.21
  117.2 6.1 %all_to_all.27 = bf16[4,1,8]{2,1,0:T(2,128)(2,1)S(1)} all-to-all(bf16[4,1,8]{2,1,0:T(2,128)(2,1)S(1)} %all_to_all.21), channel_id=1, replica_groups=mesh['rep'=8,'exp'=4] {'exp'}, dimensions={0} | all-to-all | bytes 128 | tf_op jit(solution)/shard_map/all_to_all | solution.py:79
  123.3 0.1 reshape.228
  123.3 0.1 multiply_convert_fusion.4
  123.4 0.4 convolution_bitcast_fusion.1
  123.8 0.4 convolution_bitcast_fusion
  124.2 0.4 fusion.23
  124.6 2.5 %pad_maximum_fusion = f32[1024,1152]{0,1:T(8,128)} fusion(f32[1024,384]{0,1:T(8,128)S(1)} %fusion.23, f32[1024,384]{0,1:T(8,128)S(1)} %convolution_bitcast_fusion, f32[1024,384]{0,1:T(8,128)S(1)} %convolution_bitcast_fusion.1), kind=kLoop, calls=%fused_computation.2 | loop fusion | flops 2359296 | bytes 9437184 | tf_op jit(solution)/shard_map/concatenate | solution.py:132
  127.1 0.0 reduce-scatter.2.cloned.1.call-update
  127.2 0.3 fusion.2
  127.5 1.0 fusion.1
  128.5 3.3 %all-to-all-start.2 = ((bf16[4,8,1024]{2,1,0:T(8,128)(2,1)}), bf16[4,8,1024]{2,1,0:T(8,128)(2,1)S(1)}, u32[]{:S(2)}, u32[]{:S(2)}) async-start(bf16[4,8,1024]{2,1,0:T(8,128)(2,1)} %fusion.1), calls=%async_computation.2 | async-start | bytes 131072 | tf_op jit(solution)/shard_map/all_to_all | solution.py:108
  131.8 0.1 reshape.227
  131.9 0.7 copy.51
  132.5 3.3 %all-to-all-done.2 = bf16[4,8,1024]{2,1,0:T(8,128)(2,1)S(1)} async-done(((bf16[4,8,1024]{2,1,0:T(8,128)(2,1)}), bf16[4,8,1024]{2,1,0:T(8,128)(2,1)S(1)}, u32[]{:S(2)}, u32[]{:S(2)}) %all-to-all-start.2) | async-done | bytes 65568 | tf_op jit(solution)/shard_map/all_to_all | solution.py:108
  135.9 1.0 scatter_custom_fusion
  136.9 0.7 convert_bitcast_fusion
  137.7 81.3 %reduce-scatter.2.cloned.1.call-done = f32[128,1152]{0,1:T(8,128)} async-done(((f32[1024,1152]{0,1:T(8,128)}), f32[128,1152]{0,1:T(8,128)}) %reduce-scatter.2.cloned.1.call-update) | async-done | bytes 589840 | tf_op jit(solution)/shard_map/reduce_scatter | solution.py:131
  219.0 1.2 fusion.10
  220.1 0.8 copy.54
  221.0 0.8 copy.53
  221.8 0.8 copy.52
  (33 shorter events, 0.4 us)
Async XLA Ops:
  7.2 10.0 %copy-start = (bf16[1,128,1024]{2,1,0:T(8,128)(2,1)S(1)}, bf16[1,128,1024]{2,1,0:T(8,128)(2,1)}, u32[]{:S(2)}) copy-start(bf16[1,128,1024]{2,1,0:T(8,128)(2,1)} %param.9) | copy-start | bytes 786436
  7.2 14.7 %copy-start.2 = (bf16[1,128,384]{2,1,0:T(8,128)(2,1)S(1)}, bf16[1,128,384]{2,1,0:T(8,128)(2,1)}, u32[]{:S(2)}) copy-start(bf16[1,128,384]{2,1,0:T(8,128)(2,1)} %param.12) | copy-start | bytes 294916
  7.2 46.9 %copy-start.3 = (bf16[1,128,384]{2,1,0:T(8,128)(2,1)S(1)}, bf16[1,128,384]{2,1,0:T(8,128)(2,1)}, u32[]{:S(2)}) copy-start(bf16[1,128,384]{2,1,0:T(8,128)(2,1)} %param.13) | copy-start | bytes 294916
  7.2 80.3 %collective-permute-start = (bf16[128,384]{1,0:T(8,128)(2,1)}, bf16[128,384]{1,0:T(8,128)(2,1)S(1)}, u32[]{:S(2)}, u32[]{:S(2)}) collective-permute-start(bf16[128,384]{1,0:T(8,128)(2,1)} %bitcast.102), channel_id=1, source_target_pairs={{0,4},{4,8},{8,12},{12,16},{16,20},{20,24},{24,28},{28,0},{1,5},{5... | collective-permute-start | bytes 294920 | tf_op jit(solution)/shard_map/ppermute | solution.py:18
  10.2 77.3 %collective-permute-start.1 = (bf16[128,384]{1,0:T(8,128)(2,1)}, bf16[128,384]{1,0:T(8,128)(2,1)S(1)}, u32[]{:S(2)}, u32[]{:S(2)}) collective-permute-start(bf16[128,384]{1,0:T(8,128)(2,1)} %bitcast.103), channel_id=1, source_target_pairs={{0,28},{4,0},{8,4},{12,8},{16,12},{20,16},{24,20},{28,24},{1,29},{... | collective-permute-start | bytes 294920 | tf_op jit(solution)/shard_map/ppermute | solution.py:21
  14.3 72.4 %copy-start.1 = (bf16[1,1,32,1024]{3,2,1,0:T(8,128)(2,1)S(1)}, bf16[1,1,32,1024]{3,2,1,0:T(8,128)(2,1)}, u32[]{:S(2)}) copy-start(bf16[1,1,32,1024]{3,2,1,0:T(8,128)(2,1)} %param.10) | copy-start | bytes 196612
  18.5 91.5 %all-to-all-start.1 = ((bf16[4,8,1024]{2,1,0:T(8,128)(2,1)}), bf16[4,8,1024]{2,1,0:T(8,128)(2,1)S(1)}, u32[]{:S(2)}, u32[]{:S(2)}) async-start(bf16[4,8,1024]{2,1,0:T(8,128)(2,1)} %bitcast_select_fusion), calls=%async_computation.1 | async-start | bytes 131072 | tf_op jit(solution)/shard_map/all_to_all | solution.py:72
  21.8 197.2 %reduce-scatter.2.cloned.1.call-start = ((), (), s32[]{:S(2)}) async-start(), calls=%async_computation.5 | async-start | bytes 5308416 | tf_op jit(solution)/shard_map/reduce_scatter | solution.py:131
  21.9 65.1 %copy-start.4 = (bf16[1,128,384]{2,1,0:T(8,128)(2,1)S(1)}, bf16[1,128,384]{2,1,0:T(8,128)(2,1)}, u32[]{:S(2)}) copy-start(bf16[1,128,384]{2,1,0:T(8,128)(2,1)} %param.11) | copy-start | bytes 294916
  54.1 33.1 %copy-start.5 = (bf16[1,128,8]{1,2,0:T(8,128)(2,1)S(1)}, bf16[1,128,8]{1,2,0:T(8,128)(2,1)}, u32[]{:S(2)}) copy-start(bf16[1,128,8]{1,2,0:T(8,128)(2,1)} %param.8) | copy-start | bytes 6148
  87.5 7.7 %collective-permute-start.2 = (bf16[128,384]{1,0:T(8,128)(2,1)S(1)}, bf16[128,384]{1,0:T(8,128)(2,1)S(1)}, u32[]{:S(2)}, u32[]{:S(2)}) collective-permute-start(bf16[128,384]{1,0:T(8,128)(2,1)S(1)} %collective-permute-done), channel_id=1, source_target_pairs={{0,4},{4,8},{8,12},{12,16},{16,20},{20,24},{24,28},{28,0},{1,5},{5... | collective-permute-start | bytes 294920 | tf_op jit(solution)/shard_map/ppermute | solution.py:18
  87.5 7.6 %collective-permute-start.3 = (bf16[128,384]{1,0:T(8,128)(2,1)S(1)}, bf16[128,384]{1,0:T(8,128)(2,1)S(1)}, u32[]{:S(2)}, u32[]{:S(2)}) collective-permute-start(bf16[128,384]{1,0:T(8,128)(2,1)S(1)} %collective-permute-done.1), channel_id=1, source_target_pairs={{0,28},{4,0},{8,4},{12,8},{16,12},{20,16},{24,20},{28,24},{1,29},{... | collective-permute-start | bytes 294920 | tf_op jit(solution)/shard_map/ppermute | solution.py:21
  95.1 7.3 %collective-permute-start.4 = (bf16[128,384]{1,0:T(8,128)(2,1)S(1)}, bf16[128,384]{1,0:T(8,128)(2,1)S(1)}, u32[]{:S(2)}, u32[]{:S(2)}) collective-permute-start(bf16[128,384]{1,0:T(8,128)(2,1)S(1)} %collective-permute-done.2), channel_id=1, source_target_pairs={{0,4},{4,8},{8,12},{12,16},{16,20},{20,24},{24,28},{28,0},{1,5},{5... | collective-permute-start | bytes 294920 | tf_op jit(solution)/shard_map/ppermute | solution.py:18
  95.1 7.3 %collective-permute-start.5 = (bf16[128,384]{1,0:T(8,128)(2,1)S(1)}, bf16[128,384]{1,0:T(8,128)(2,1)S(1)}, u32[]{:S(2)}, u32[]{:S(2)}) collective-permute-start(bf16[128,384]{1,0:T(8,128)(2,1)S(1)} %collective-permute-done.3), channel_id=1, source_target_pairs={{0,28},{4,0},{8,4},{12,8},{16,12},{20,16},{24,20},{28,24},{1,29},{... | collective-permute-start | bytes 294920 | tf_op jit(solution)/shard_map/ppermute | solution.py:21
  102.5 7.3 %collective-permute-start.6 = (bf16[128,384]{1,0:T(8,128)(2,1)S(1)}, bf16[128,384]{1,0:T(8,128)(2,1)S(1)}, u32[]{:S(2)}, u32[]{:S(2)}) collective-permute-start(bf16[128,384]{1,0:T(8,128)(2,1)S(1)} %collective-permute-done.4), channel_id=1, source_target_pairs={{0,4},{4,8},{8,12},{12,16},{16,20},{20,24},{24,28},{28,0},{1,5},{5... | collective-permute-start | bytes 294920 | tf_op jit(solution)/shard_map/ppermute | solution.py:18
  128.5 7.4 %all-to-all-start.2 = ((bf16[4,8,1024]{2,1,0:T(8,128)(2,1)}), bf16[4,8,1024]{2,1,0:T(8,128)(2,1)S(1)}, u32[]{:S(2)}, u32[]{:S(2)}) async-start(bf16[4,8,1024]{2,1,0:T(8,128)(2,1)} %fusion.1), calls=%async_computation.2 | async-start | bytes 131072 | tf_op jit(solution)/shard_map/all_to_all | solution.py:108
Sparse Core Ops, SparseCore 0:
  127.3 91.6 reduce-scatter.1
